TPU v7x, 32 devices: a whole 2x2x4 slice. The times are simulated.
32 devices in a mesh: dp: 8 (over z, x), gate: 4 (over y, core).
Axes of the slice: x: 2, y: 2, z: 4, core: 2. Of those that a mesh axis runs over, the one named last changes fastest.
Arguments:
- inputs: bfloat16 [8, 2048, 2048], P('dp'), may hold values from -6 to 6
- weight: bfloat16 [2048, 6144], P(None, 'gate'), may hold values from -0.125 to 0.125
- ln_gain: float32 [2048], replicated, may hold values from 0.5 to 1.5
- ln_bias: float32 [2048], replicated, may hold values from -3 to 3
- forget_peep: float32 [2048], P('gate'), may hold values from -1 to 1
- reset_peep: float32 [2048], P('gate'), may hold values from -1 to 1
- forget_bias: float32 [2048], P('gate'), may hold values from 0 to 8
- reset_bias: float32 [2048], P('gate'), may hold values from -1 to 1
- resets: int32 [8, 2048], P('dp'), may hold values from 0 to 1, as said below
- padding: int32 [8, 2048], P('dp'), may hold values from 0 to 1, as said below
- grad_out: bfloat16 [8, 2048, 2048], P('dp', None, 'gate'), may hold values from -6 to 6
Outputs:
- hidden_out: bfloat16 [8, 2048, 2048], P('dp', None, 'gate')
- grad_inputs: bfloat16 [8, 2048, 2048], P('dp', None, 'gate')
- grad_weight: float32 [2048, 6144], P(None, 'gate')
- grad_ln_gain: float32 [2048], P('gate')
- grad_ln_bias: float32 [2048], P('gate')
- grad_forget_peep: float32 [2048], P('gate')
- grad_reset_peep: float32 [2048], P('gate')
- grad_forget_bias: float32 [2048], P('gate')
- grad_reset_bias: float32 [2048], P('gate')
Inputs may be any that keep to these rules, and one draw needn't show every extreme that they name: `padding`: each row holds ones followed by zeros, with more than 1536 ones; row 0 is all ones. `resets`: position 0 of every row is 1; row 0 has no other ones.
All inputs are finite; a program needn't handle non-finite values.
Results may differ from a plain program's by a relative error of at most 0.0065.
Values may be sent and summed in bfloat16 or wider, within the bound.
No kernel may reach another device: no remote copies, remote signals or barrier semaphores. Data moves between devices by JAX's collectives and lax.ppermute only.
A program may use at most 192 MiB of HBM per device.

v0:
```python
import math
import jax
import jax.numpy as jnp
from jax import lax
from jax.sharding import PartitionSpec as P

epsilon = 1e-05


def combine(earlier, later):
    early_decay, early_drive = earlier
    late_decay, late_drive = later
    return (early_decay * late_decay, late_decay * early_drive + late_drive)


def chained(decays, drives, backward):
    rows, length, channels = decays.shape
    span = math.gcd(length, 16)
    count = length // span
    dec_blocks = decays.reshape(rows, count, span, channels).transpose(2, 0, 1, 3)
    drv_blocks = drives.reshape(rows, count, span, channels).transpose(2, 0, 1, 3)
    order = list(range(span))
    if backward:
        order = order[::-1]
    run_decay = jnp.ones((rows, count, channels), jnp.float32)
    run_drive = jnp.zeros((rows, count, channels), jnp.float32)
    part_decay = [None] * span
    part_drive = [None] * span
    for step in order:
        run_decay = dec_blocks[step] * run_decay
        run_drive = dec_blocks[step] * run_drive + drv_blocks[step]
        part_decay[step] = run_decay
        part_drive[step] = run_drive
    inclusive = lax.associative_scan(combine, (run_decay, run_drive), reverse=backward, axis=1)[1]
    edge = jnp.zeros((rows, 1, channels), jnp.float32)
    if backward:
        incoming = jnp.concatenate([inclusive[:, 1:], edge], axis=1)
    else:
        incoming = jnp.concatenate([edge, inclusive[:, :-1]], axis=1)
    states = jnp.stack(
        [part_drive[step] + part_decay[step] * incoming for step in range(span)], axis=0
    )
    return states.transpose(1, 2, 0, 3).reshape(rows, length, channels)


def contract(left, right, left_dim, right_dim):
    return lax.dot_general(
        left, right, (((left_dim,), (right_dim,)), ((), ())), preferred_element_type=jnp.float32
    )


def shards(
    inputs,
    weight,
    ln_gain,
    ln_bias,
    forget_peep,
    reset_peep,
    forget_bias,
    reset_bias,
    resets,
    padding,
    grad_out,
):
    rows, length, features = inputs.shape
    tokens = rows * length
    channels = forget_peep.shape[0]
    offset = lax.axis_index("gate") * channels
    flat_rows = inputs.astype(jnp.float32).reshape(tokens, features)
    row_mean = jnp.mean(flat_rows, axis=1, keepdims=True)
    centered = flat_rows - row_mean
    inv_std = lax.rsqrt(jnp.mean(centered * centered, axis=1, keepdims=True) + epsilon)
    unit_rows = centered * inv_std
    normed = (unit_rows * ln_gain + ln_bias).astype(jnp.bfloat16)
    local_cols = jnp.dot(normed, weight, preferred_element_type=jnp.float32).astype(jnp.bfloat16)
    mixed_cols = lax.all_to_all(local_cols, "gate", split_axis=1, concat_axis=1, tiled=True)
    utilde = mixed_cols[:, :channels].astype(jnp.float32).reshape(rows, length, channels)
    uforget = (
        mixed_cols[:, channels : 2 * channels].astype(jnp.float32).reshape(rows, length, channels)
    )
    ureset = mixed_cols[:, 2 * channels :].astype(jnp.float32).reshape(rows, length, channels)
    xslice = lax.dynamic_slice_in_dim(inputs, offset, channels, 2).astype(jnp.float32)
    forget = jax.nn.sigmoid(uforget + forget_peep * xslice + forget_bias)
    reset_gate = jax.nn.sigmoid(ureset + reset_peep * xslice + reset_bias)
    carry_keep = (1 - resets).astype(jnp.float32)[:, :, None]
    decays = forget * carry_keep
    drives = (1.0 - forget) * utilde
    memory = chained(decays, drives, False)
    live_mask = padding.astype(jnp.float32)[:, :, None]
    outputs = live_mask * (reset_gate * memory + (1.0 - reset_gate) * xslice)
    grad_live = grad_out.astype(jnp.float32) * live_mask
    dreset = grad_live * (memory - xslice) * reset_gate * (1.0 - reset_gate)
    dcell_local = grad_live * reset_gate
    edge_zeros = jnp.zeros((rows, 1, channels), jnp.float32)
    decay_next = jnp.concatenate([decays[:, 1:], edge_zeros], axis=1)
    dcells = chained(decay_next, dcell_local, True)
    previous = jnp.concatenate([edge_zeros, memory[:, :-1]], axis=1)
    dtilde = dcells * (1.0 - forget)
    dforget = dcells * (previous * carry_keep - utilde) * forget * (1.0 - forget)
    direct = grad_live * (1.0 - reset_gate) + dforget * forget_peep + dreset * reset_peep
    dstreams = (
        jnp.concatenate([dtilde, dforget, dreset], axis=2)
        .reshape(tokens, 3 * channels)
        .astype(jnp.bfloat16)
    )
    dlocal = lax.all_to_all(dstreams, "gate", split_axis=1, concat_axis=1, tiled=True)
    partial_in = contract(dlocal, weight, 1, 1)
    weight_grad = contract(normed, dlocal, 0, 0)
    dnormed = lax.psum_scatter(partial_in, "gate", scatter_dimension=1, tiled=True)
    unit_slice = lax.dynamic_slice_in_dim(unit_rows, offset, channels, 1)
    gain_slice = lax.dynamic_slice_in_dim(ln_gain, offset, channels, 0)
    grad_unit = dnormed * gain_slice
    first_total, second_total = lax.psum(
        (
            jnp.sum(grad_unit, axis=1, keepdims=True),
            jnp.sum(grad_unit * unit_slice, axis=1, keepdims=True),
        ),
        "gate",
    )
    dx_norm = inv_std * (grad_unit - first_total / features - unit_slice * second_total / features)
    dinputs = (
        (dx_norm + direct.reshape(tokens, channels))
        .astype(jnp.bfloat16)
        .reshape(rows, length, channels)
    )
    totals = lax.psum(
        (
            weight_grad,
            jnp.sum(dnormed * unit_slice, axis=0),
            jnp.sum(dnormed, axis=0),
            jnp.sum(dforget * xslice, axis=(0, 1)),
            jnp.sum(dreset * xslice, axis=(0, 1)),
            jnp.sum(dforget, axis=(0, 1)),
            jnp.sum(dreset, axis=(0, 1)),
        ),
        "dp",
    )
    return (
        outputs.astype(jnp.bfloat16),
        dinputs,
        totals[0],
        totals[1],
        totals[2],
        totals[3],
        totals[4],
        totals[5],
        totals[6],
    )


def solution(mesh):
    return jax.shard_map(
        shards,
        mesh=mesh,
        in_specs=(
            P("dp", None, None),
            P(None, "gate"),
            P(),
            P(),
            P("gate"),
            P("gate"),
            P("gate"),
            P("gate"),
            P("dp", None),
            P("dp", None),
            P("dp", None, "gate"),
        ),
        out_specs=(
            P("dp", None, "gate"),
            P("dp", None, "gate"),
            P(None, "gate"),
            P("gate"),
            P("gate"),
            P("gate"),
            P("gate"),
            P("gate"),
            P("gate"),
        ),
        check_vma=False,
    )
```

profile of v0, /device:TPU:0, one launch (start us, length us, event | category | flops | bytes accessed | tf_op | source)
XLA Modules:
  0.0 1001.1 jit_solution(17736742718394757281)
XLA Ops:
  8.0 4.7 convert_reduce_fusion
  13.8 2.3 fusion.3
  16.6 18.4 %fusion.18 = bf16[2048,1536]{0,1:T(8,128)(2,1)} fusion(bf16[2048,1536]{1,0:T(8,128)(2,1)S(1)} %copy-done.59, f32[2048]{0:T(1024)S(1)} %copy-done.60, f32[2048]{0:T(1024)S(1)} %copy-done.57, bf16[1,2048,2048]{2,1,0:T(8,128)(2,1)} %param.11, f32[2048]{0:T(1024)S(1)} %add_rsqrt_fusion, f32[2048]{0:T(1024)S(1)} %broadcast_multiply_fusion.2), kind=kOutput, calls=%fused_computation.27 | convolution fusion | flops 12913213440 | bytes 21004288 | tf_op jit(solution)/shard_map/dot_general | solution.py:75
  35.0 5.4 all-to-all-start
  40.6 71.2 %all-to-all-done = bf16[2048,4,384]{0,2,1:T(8,128)(2,1)} async-done(((bf16[2048,4,384]{0,2,1:T(8,128)(2,1)}), bf16[2048,4,384]{0,2,1:T(8,128)(2,1)}, u32[]{:S(2)}, u32[]{:S(2)}) %all-to-all-start) | async-done | bytes 6291488 | tf_op jit(solution)/shard_map/all_to_all | solution.py:76
  111.8 5.8 fusion.153
  117.6 3.1 copy.28
  120.7 3.9 copy.29
  124.6 3.9 copy.30
  128.6 7.4 convert_multiply_fusion.5
  136.5 1.5 copy-done.1
  138.5 4.3 fusion.93
  142.8 15.9 %fusion.46 = (f32[1,128,512]{2,0,1:T(1,128)S(1)}, f32[1,128,512]{2,0,1:T(1,128)}, f32[1,128,512]{2,0,1:T(1,128)}, f32[1,128,512]{2,0,1:T(1,128)}, f32[1,128,512]...) fusion(f32[16,1,128,512]{3,0,2,1:T(8,128)} %bitcast.786, ...), kind=kLoop, calls=%fused_computation.66 | loop fusion | flops 2097152 | bytes 10485760 | tf_op jit(solution)/shard_map/add | solution.py:31
  164.5 16.6 %fusion.78 = (f32[1,128,512]{2,0,1:T(1,128)S(1)}, f32[1,128,512]{2,0,1:T(1,128)}, f32[1,128,512]{2,0,1:T(1,128)}, f32[1,128,512]{2,0,1:T(1,128)}, f32[1,128,512]...) fusion(f32[16,1,128,512]{3,0,2,1:T(8,128)} %bitcast.771), kind=kLoop, calls=%fused_computation.193 | loop fusion | flops 983040 | bytes 6029312 | tf_op jit(solution)/shard_map/mul | solution.py:30
  181.1 16.4 %fusion.62 = (f32[1,128,512]{2,0,1:T(1,128)S(1)}, f32[1,128,512]{2,0,1:T(1,128)}, f32[1,128,512]{2,0,1:T(1,128)}, f32[1,128,512]{2,0,1:T(1,128)}, f32[1,128,512]...) fusion(f32[16,1,128,512]{3,0,2,1:T(8,128)} %bitcast.782, ...), kind=kLoop, calls=%fused_computation.114 | loop fusion | flops 2097152 | bytes 10485760 | tf_op jit(solution)/shard_map/add | solution.py:31
  200.5 1.9 pad.92
  202.4 1.9 pad.93
  205.6 1.3 fusion.117
  208.7 1.4 pad.95
  211.4 3.2 pad.94
  215.4 1.3 add.1721
  217.4 3.0 pad.96
  220.4 4.5 pad.97
  225.0 1.4 add.1723
  226.4 1.4 fusion.113
  227.8 5.6 pad.99
  233.4 1.4 pad_maximum_fusion.5
  234.8 5.5 pad.98
  241.6 11.0 %pad.101 = f32[1,64,512]{2,0,1:T(1,128)S(1)} pad(f32[1,32,512]{2,0,1:T(1,128)} %add.1725, f32[]{:T(128)} %constant.10.clone.1), padding=0_0_0x1_0_1x0_0_0 | pad | bytes 196612 | tf_op jit(solution)/shard_map/pad | solution.py:34
  255.0 11.0 %pad.115 = f32[1,64,512]{2,0,1:T(1,128)S(1)} pad(f32[1,32,512]{2,0,1:T(1,128)} %add.1778, f32[]{:T(128)} %constant.10.clone.1), padding=0_0_0x1_0_1x0_0_0 | pad | bytes 196612 | tf_op jit(solution)/shard_map/pad | solution.py:34
  266.7 28.5 %pad.211 = f32[1,128,512]{2,0,1:T(1,128)} pad(f32[1,64,512]{2,0,1:T(1,128)} %add.1780, f32[]{:T(128)} %constant.10.clone.1), padding=0_0_0x1_0_1x0_0_0 | pad | bytes 393220
  297.2 21.9 %pad.149 = f32[1,127,512]{2,0,1:T(1,128)S(1)} pad(f32[1,64,512]{2,0,1:T(1,128)} %pad_maximum_fusion.2, f32[]{:T(128)} %constant.10.clone.1), padding=0_0_0x0_0_1x0_0_0 | pad | bytes 391172 | tf_op jit(solution)/shard_map/slice | solution.py:37
  319.1 1.9 slice_add_fusion.15
  322.1 19.8 %pad.210 = f32[1,128,512]{2,0,1:T(1,128)} pad(f32[1,64,512]{2,0,1:T(1,128)S(1)} %add.1727, f32[]{:T(128)} %constant.10.clone.1), padding=0_0_0x1_0_1x0_0_0 | pad | bytes 393220
  342.9 19.8 %pad.147 = f32[1,127,512]{2,0,1:T(1,128)} pad(f32[1,64,512]{2,0,1:T(1,128)S(1)} %pad_maximum_fusion.1, f32[]{:T(128)} %constant.10.clone.1), padding=0_0_0x0_0_1x0_0_0 | pad | bytes 391172 | tf_op jit(solution)/shard_map/slice | solution.py:39
  362.7 1.4 slice_add_fusion.16
  364.1 7.0 add_bitcast_fusion.17
  371.2 3.3 add_bitcast_fusion.16
  374.6 3.2 add_bitcast_fusion.18
  377.8 5.1 add_bitcast_fusion.19
  383.0 3.1 add_bitcast_fusion.4
  386.2 2.4 add_bitcast_fusion.3
  388.6 3.2 add_bitcast_fusion
  391.8 3.2 add_bitcast_fusion.10
  395.1 4.3 add_bitcast_fusion.21
  399.4 13.4 %stack.135 = f32[16,1,128,512]{3,0,2,1:T(8,128)} concatenate(f32[1,1,128,512]{3,0,2,1:T(1,128)} %get-tuple-element.134, f32[1,1,128,512]{3,0,2,1:T(1,128)} %get-tuple-element.68, f32[1,1,128,512]{3,0,2,1:T(1,128)} %get-tuple-element.83, f32[1,1,128,512]{3,0,2,1:T(1,128)} %get-tuple-element.65, f32[1,1,128,512]{3,0,2,1:T(1,128)} %get-tuple-element.93, ...), dimensions={0} | concatenate | bytes 8388608 | tf_op jit(solution)/shard_map/stack | solution.py:40
  412.9 12.9 %stack.118 = f32[16,1,128,512]{3,0,2,1:T(8,128)} concatenate(f32[1,1,128,512]{3,0,2,1:T(1,128)} %get-tuple-element.76, f32[1,1,128,512]{3,0,2,1:T(1,128)} %get-tuple-element.82, f32[1,1,128,512]{3,0,2,1:T(1,128)} %get-tuple-element.73, f32[1,1,128,512]{3,0,2,1:T(1,128)S(1)} %copy-done.34, f32[1,1,128,512]{3,0,2,1:T(1,128)S(1)} %copy-done.32, ...), dimensions={0} | concatenate | bytes 8388608 | tf_op jit(solution)/shard_map/stack | solution.py:40
  425.8 11.7 %fusion.41 = (f32[512]{0:T(512)S(1)}, f32[512]{0:T(512)S(1)}, f32[512]{0:T(512)S(1)}, f32[512]{0:T(512)S(1)}, f32[1,2048,512]{2,1,0:T(8,128)S(1)}, /*index=5*/f3...) fusion(bf16[1,2048,2048]{2,1,0:T(8,128)(2,1)} %param.11, s32[]{:T(128)S(6)} %select_n.2, ...), kind=kLoop, calls=%fused_computation.53 | loop fusion | flops 44038144 | bytes 35682308 | tf_op jit(solution)/shard_map/reduce_sum | solution.py:132
  438.2 1.5 copy-done.6
  440.8 2.9 pad_maximum_fusion
  443.8 11.4 %convert_element_type.48 = bf16[2048,4,384]{2,1,0:T(4,128)(2,1)} reshape(bf16[1,2048,1536]{2,1,0:T(8,128)(2,1)} %pad_maximum_fusion) | data formatting | bytes 12582912 | tf_op jit(solution)/shard_map/convert_element_type | solution.py:104
  455.1 3.6 copy.25
  458.7 74.4 %all_to_all.21 = bf16[2048,4,384]{2,0,1:T(8,128)(2,1)} all-to-all(bf16[2048,4,384]{2,0,1:T(8,128)(2,1)S(1)} %copy.25), channel_id=1, replica_groups=mesh['dp'=8,'gate'=4] {'gate'}, dimensions={1} | all-to-all | bytes 12582912 | tf_op jit(solution)/shard_map/all_to_all | solution.py:106
  533.2 8.7 copy.26
  541.8 20.5 %fusion.160 = f32[2048,2048]{1,0:T(8,128)} fusion(bf16[2048,1536]{0,1:T(8,128)(2,1)} %bitcast.791, bf16[2048,1536]{1,0:T(8,128)(2,1)} %param.12), kind=kOutput, calls=%fused_computation.308 | convolution fusion | flops 12884901888 | bytes 29360128 | tf_op jit(solution)/shard_map/dot_general | solution.py:47
  563.1 23.3 %fusion.10 = f32[2048,1536]{1,0:T(8,128)} fusion(bf16[2048,1536]{0,1:T(8,128)(2,1)} %bitcast.792, bf16[1,2048,2048]{2,1,0:T(8,128)(2,1)} %param.11, f32[2048]{0:T(1024)S(1)} %copy-done.61, f32[2048]{0:T(1024)S(1)} %copy-done.58, f32[2048]{0:T(1024)S(1)} %copy-done.41, f32[2048]{0:T(1024)S(1)} %copy-done.43), kind=kOutput, calls=%fused_computation.20 | convolution fusion | flops 12910067712 | bytes 27295744 | tf_op jit(solution)/shard_map/dot_general | solution.py:47
  586.5 12.6 %fusion.1 = f32[2048,2048]{1,0:T(8,128)} fusion(bf16[1,2048,2048]{2,1,0:T(8,128)(2,1)} %param.11, f32[2048]{0:T(1024)S(1)} %copy-done.41, f32[2048]{0:T(1024)S(1)} %copy-done.43), kind=kLoop, calls=%fused_computation.4 | loop fusion | flops 12582912 | bytes 25182208 | tf_op jit(solution)/shard_map/mul | solution.py:73
  599.1 89.5 %reduce-scatter.2.cloned.1.call-done = f32[2048,512]{1,0:T(8,128)} async-done(((f32[2048,2048]{1,0:T(8,128)}), f32[2048,512]{1,0:T(8,128)}) %reduce-scatter.2.cloned.1.call-update) | async-done | bytes 4194320 | tf_op jit(solution)/shard_map/reduce_scatter | solution.py:109
  688.6 5.1 multiply_reduce_fusion
  693.7 39.1 %all-reduce.32 = (f32[512]{0:T(512)}, f32[512]{0:T(512)}, f32[512]{0:T(512)}, f32[512]{0:T(512)}, f32[512]{0:T(512)}, /*index=5*/f32[512]{0:T(512)}) all-reduce(f32[512]{0:T(512)S(1)} %get-tuple-element.9, f32[512]{0:T(512)S(1)} %get-tuple-element.16, f32[512]{0:T(512)S(1)} %get-tuple-element.12, ...), channel_id=1, replica_groups=mesh['dp'=8,'gate'=4] {'dp'}, use_global_device_ids=true, to_apply=%region_9.0 | all-reduce | flops 3072 | bytes 24576 | tf_op jit(solution)/shard_map/psum | solution.py:126
  732.8 10.6 %all-reduce.33 = (f32[2048]{0:T(1024)S(1)}, f32[2048,1]{0,1:T(1,128)S(1)}) all-reduce(f32[2048]{0:T(1024)S(1)} %get-tuple-element.10, f32[2048,1]{0,1:T(1,128)S(1)} %bitcast.799), channel_id=1, replica_groups=mesh['dp'=8,'gate'=4] {'gate'}, use_global_device_ids=true, to_apply=%region_6.0 | all-reduce | flops 4096 | bytes 32768 | tf_op jit(solution)/shard_map/psum | solution.py:113
  743.3 10.2 %fusion.45 = bf16[1,2048,512]{2,1,0:T(8,128)(2,1)} fusion(f32[1,2048,512]{2,1,0:T(8,128)} %copy-done.7, f32[512]{0:T(512)S(1)} %copy-done.51, f32[1,2048,512]{2,1,0:T(8,128)} %copy-done.6, f32[512]{0:T(512)S(1)} %copy-done.47, f32[2048]{0:T(1024)S(1)} %bitcast.795, bf16[1,2048,512]{2,1,0:T(8,128)(2,1)} %param.21, f32[2048]{0:T(1024)S(1)} %get-tuple-element.23, ...), kind=kLoop, calls=%fused_computation.64 | loop fusion | flops 25165824 | bytes 25206788 | tf_op jit(solution)/shard_map/reshape | solution.py:124
  753.5 229.0 %all-reduce.36.cloned.1.call-done = f32[2048,1536]{1,0:T(8,128)} async-done(((f32[2048,1536]{1,0:T(8,128)}), f32[2048,1536]{1,0:T(8,128)}) %all-reduce.36.cloned.1.call-update) | async-done | bytes 12582928 | tf_op jit(solution)/shard_map/psum | solution.py:126
  982.6 10.6 %copy.32 = f32[2048,1536]{1,0:T(8,128)} copy(f32[2048,1536]{1,0:T(8,128)} %all-reduce.36.cloned.1.call-done) | data formatting | bytes 25165824
  (206 shorter events, 28.3 us)
Async XLA Ops:
  8.0 5.8 copy-start
  13.8 2.3 copy-start.42
  13.8 2.4 copy-start.57
  13.8 2.8 copy-start.59
  13.8 2.8 copy-start.60
  16.6 18.4 %copy-start.40 = (f32[2048]{0:T(1024)}, f32[2048]{0:T(1024)S(1)}, u32[]{:S(2)}) copy-start(f32[2048]{0:T(1024)S(1)} %add_rsqrt_fusion) | copy-start | bytes 24580
  35.0 5.5 copy-start.53
  35.0 5.5 copy-start.54
  35.0 76.8 %all-to-all-start = ((bf16[2048,4,384]{0,2,1:T(8,128)(2,1)}), bf16[2048,4,384]{0,2,1:T(8,128)(2,1)}, u32[]{:S(2)}, u32[]{:S(2)}) async-start(bf16[2048,4,384]{0,2,1:T(8,128)(2,1)} %bitcast.790), calls=%async_computation | async-start | bytes 12582912 | tf_op jit(solution)/shard_map/all_to_all | solution.py:76
  40.4 648.1 %reduce-scatter.2.cloned.1.call-start = ((), (), s32[]{:S(2)}) async-start(), calls=%async_computation.3 | async-start | bytes 20971520 | tf_op jit(solution)/shard_map/reduce_scatter | solution.py:109
  40.5 88.0 %copy-start.37 = (f32[1,2048]{1,0:T(1,128)}, f32[1,2048]{1,0:T(1,128)S(1)}, u32[]{:S(2)}) copy-start(f32[1,2048]{1,0:T(1,128)S(1)} %convert_element_type.40) | copy-start | bytes 24580
  40.6 88.0 %copy-start.44 = (f32[1,2048]{1,0:T(1,128)}, f32[1,2048]{1,0:T(1,128)S(1)}, u32[]{:S(2)}) copy-start(f32[1,2048]{1,0:T(1,128)S(1)} %subtract_convert_fusion) | copy-start | bytes 24580
  120.7 7.9 copy-start.46
  120.7 7.9 copy-start.48
  120.7 7.9 copy-start.50
  120.7 7.9 copy-start.55
  136.0 2.1 copy-start.1
  138.5 20.2 %copy-start.4 = (f32[1,2048,512]{2,1,0:T(8,128)}, f32[1,2048,512]{2,1,0:T(8,128)S(1)}, u32[]{:S(2)}) copy-start(f32[1,2048,512]{2,1,0:T(8,128)S(1)} %concatenate.59) | copy-start | bytes 12582916
  161.2 19.9 %copy-start.2 = (f32[1,2048,512]{2,1,0:T(8,128)S(1)}, f32[1,2048,512]{2,1,0:T(8,128)}, u32[]{:S(2)}) copy-start(f32[1,2048,512]{2,1,0:T(8,128)} %copy-done.1) | copy-start | bytes 12582916
  198.0 0.6 copy-start.36
  198.6 0.6 copy-start.39
  220.4 76.0 %copy-start.52 = (f32[1,1,512]{2,0,1:T(1,128)S(1)}, f32[1,1,512]{2,0,1:T(1,128)}, u32[]{:S(2)}) copy-start(f32[1,1,512]{2,0,1:T(1,128)} %slice.857) | copy-start | bytes 6148
  362.6 8.6 copy-start.19
  362.7 8.6 copy-start.20
  362.7 8.6 copy-start.21
  362.7 8.6 copy-start.22
  362.7 8.6 copy-start.23
  364.1 18.8 %copy-start.8 = (f32[1,2048,512]{2,1,0:T(8,128)S(1)}, f32[1,2048,512]{2,1,0:T(8,128)}, u32[]{:S(2)}) copy-start(f32[1,2048,512]{2,1,0:T(8,128)} %get-tuple-element.77) | copy-start | bytes 12582916
  371.2 6.6 copy-start.3
  371.2 6.6 copy-start.18
  374.5 8.4 copy-start.5
  374.5 8.4 copy-start.12
  374.5 8.4 copy-start.13
  374.5 8.4 copy-start.14
  374.5 8.4 copy-start.15
  374.6 8.4 copy-start.16
  374.6 8.4 copy-start.17
  377.8 8.4 copy-start.9
  377.8 8.4 copy-start.10
  382.9 5.7 copy-start.11
  382.9 5.7 copy-start.26
  382.9 5.7 copy-start.27
  386.2 5.7 copy-start.24
  386.2 5.7 copy-start.25
  388.6 6.5 copy-start.28
  388.6 6.5 copy-start.29
  399.4 13.4 %copy-start.30 = (f32[1,1,128,512]{3,0,2,1:T(1,128)S(1)}, f32[1,1,128,512]{3,0,2,1:T(1,128)}, u32[]{:S(2)}) copy-start(f32[1,1,128,512]{3,0,2,1:T(1,128)} %get-tuple-element.69) | copy-start | bytes 786436
  399.4 13.4 %copy-start.31 = (f32[1,1,128,512]{3,0,2,1:T(1,128)S(1)}, f32[1,1,128,512]{3,0,2,1:T(1,128)}, u32[]{:S(2)}) copy-start(f32[1,1,128,512]{3,0,2,1:T(1,128)} %get-tuple-element.70) | copy-start | bytes 786436
  399.4 13.4 %copy-start.32 = (f32[1,1,128,512]{3,0,2,1:T(1,128)S(1)}, f32[1,1,128,512]{3,0,2,1:T(1,128)}, u32[]{:S(2)}) copy-start(f32[1,1,128,512]{3,0,2,1:T(1,128)} %get-tuple-element.71) | copy-start | bytes 786436
  399.4 13.4 %copy-start.33 = (f32[1,1,128,512]{3,0,2,1:T(1,128)S(1)}, f32[1,1,128,512]{3,0,2,1:T(1,128)}, u32[]{:S(2)}) copy-start(f32[1,1,128,512]{3,0,2,1:T(1,128)} %get-tuple-element.96) | copy-start | bytes 786436
  399.4 13.4 %copy-start.34 = (f32[1,1,128,512]{3,0,2,1:T(1,128)S(1)}, f32[1,1,128,512]{3,0,2,1:T(1,128)}, u32[]{:S(2)}) copy-start(f32[1,1,128,512]{3,0,2,1:T(1,128)} %get-tuple-element.97) | copy-start | bytes 786436
  412.9 12.9 %copy-start.38 = (f32[1,2048]{1,0:T(1,128)S(1)}, f32[1,2048]{1,0:T(1,128)}, u32[]{:S(2)}) copy-start(f32[1,2048]{1,0:T(1,128)} %copy-done.37) | copy-start | bytes 24580
  412.9 12.9 %copy-start.45 = (f32[1,2048]{1,0:T(1,128)S(1)}, f32[1,2048]{1,0:T(1,128)}, u32[]{:S(2)}) copy-start(f32[1,2048]{1,0:T(1,128)} %copy-done.44) | copy-start | bytes 24580
  412.9 12.9 %copy-start.47 = (f32[512]{0:T(512)S(1)}, f32[512]{0:T(512)}, u32[]{:S(2)}) copy-start(f32[512]{0:T(512)} %param.15) | copy-start | bytes 6148
  412.9 12.9 %copy-start.49 = (f32[512]{0:T(512)S(1)}, f32[512]{0:T(512)}, u32[]{:S(2)}) copy-start(f32[512]{0:T(512)} %param.18) | copy-start | bytes 6148
  412.9 12.9 %copy-start.51 = (f32[512]{0:T(512)S(1)}, f32[512]{0:T(512)}, u32[]{:S(2)}) copy-start(f32[512]{0:T(512)} %param.16) | copy-start | bytes 6148
  412.9 12.9 %copy-start.56 = (f32[512]{0:T(512)S(1)}, f32[512]{0:T(512)}, u32[]{:S(2)}) copy-start(f32[512]{0:T(512)} %param.17) | copy-start | bytes 6148
  437.6 2.1 copy-start.6
  437.6 3.2 copy-start.7
  562.4 0.7 copy-start.41
  562.4 0.7 copy-start.43
  562.4 0.7 copy-start.58
  562.4 0.7 copy-start.61
  562.4 420.1 %all-reduce.36.cloned.1.call-start = ((), (), s32[]{:S(2)}) async-start(), calls=%async_computation.4 | async-start | bytes 25165824 | tf_op jit(solution)/shard_map/psum | solution.py:126
  (1 other events, 0.6 us)
Sparse Core Ops, SparseCore 0:
  562.6 125.9 reduce-scatter.1
Sparse Core Ops, SparseCore 1:
  586.5 396.0 all-reduce.35
where the time goes:
time: 1020 us; the launch traced here: 1000 us
  waiting for transfers between devices  390 us (38%)
  local copies, waits for them, and re-layouts  232 us (23%)
  other arithmetic  170 us (17%)
  blocking collectives  124 us (12%)
  matrix products  62.2 us (6%)
  between operations  17 us (2%)
    psum x1, waiting for transfers between devices, shards(): lax.psum((weight_grad, jnp.sum(dnormed * unit_slice, axis=0), jnp.sum(dno...  229 us
    reduce_scatter x1, waiting for transfers between devices, shards(): lax.psum_scatter(partial_in, 'gate', scatter_dimension=1, tiled=True)  89.5 us
    unnamed x130, local copies, waits for them, and re-layouts  77.5 us
    all_to_all x1, blocking collectives, shards(): lax.all_to_all(dstreams, 'gate', split_axis=1, concat_axis=1, tiled=True)  74.4 us
    all_to_all x1, waiting for transfers between devices, shards(): lax.all_to_all(local_cols, 'gate', split_axis=1, concat_axis=1, tiled=True)  71.2 us
    pad x20, local copies, waits for them, and re-layouts, chained(): lax.associative_scan(combine, (run_decay, run_drive), reverse=backward, a...  50.7 us
    dot_general x2, matrix products, contract(): lax.dot_general(left, right, (((left_dim,), (right_dim,)), ((), ())), pre...  43.8 us
    psum x1, blocking collectives, shards(): lax.psum((weight_grad, jnp.sum(dnormed * unit_slice, axis=0), jnp.sum(dno...  39.1 us
  transfers between devices with their start and end apart: 3, of which 3 were waited for; matrix products, arithmetic and copies ran while one was open for 5% of the time, Pallas kernels for 0%

commit v1 on v0

--- a/solution.py
+++ b/solution.py
@@ -5,6 +5,22 @@
 from jax.sharding import PartitionSpec as P
 
 epsilon = 1e-05
+
+
+def exchange_in_pairs(x, axis, split, join):
+    ways, here = (lax.axis_size(axis), lax.axis_index(axis))
+    width = x.shape[split] // ways
+    lengths = list(x.shape)
+    lengths[split] = width
+    height = lengths[join]
+    lengths[join] = height * ways
+    full = jnp.zeros(lengths, x.dtype)
+    for mask in range(ways):
+        part = lax.dynamic_slice_in_dim(x, (here ^ mask) * width, width, axis=split)
+        if mask:
+            part = lax.ppermute(part, axis, [(d, d ^ mask) for d in range(ways)])
+        full = lax.dynamic_update_slice_in_dim(full, part, (here ^ mask) * height, axis=join)
+    return full
 
 
 def combine(earlier, later):
@@ -73,7 +89,7 @@
     unit_rows = centered * inv_std
     normed = (unit_rows * ln_gain + ln_bias).astype(jnp.bfloat16)
     local_cols = jnp.dot(normed, weight, preferred_element_type=jnp.float32).astype(jnp.bfloat16)
-    mixed_cols = lax.all_to_all(local_cols, "gate", split_axis=1, concat_axis=1, tiled=True)
+    mixed_cols = exchange_in_pairs(local_cols, "gate", 1, 1)
     utilde = mixed_cols[:, :channels].astype(jnp.float32).reshape(rows, length, channels)
     uforget = (
         mixed_cols[:, channels : 2 * channels].astype(jnp.float32).reshape(rows, length, channels)

time: 1020 us -> 888 us (0.87); the launches traced: 1000 us -> 882 us
  local copies, waits for them, and re-layouts: 232 us -> 146 us
  other arithmetic: 170 us -> 148 us
    all_to_all x1 -> x0, waiting for transfers between devices: 71.2 us -> none  [shards(): lax.all_to_all(local_cols, 'gate', split_axis=1, concat_axis=1, tiled=True)]
    ppermute x0 -> x3, waiting for transfers between devices: none -> 64.2 us  [exchange_in_pairs(): part = lax.ppermute(part, axis, [(d, d ^ mask) for d in range(ways)])]
    pad x20, local copies, waits for them, and re-layouts: 50.7 us -> 3.52 us  [chained(): lax.associative_scan(combine, (run_decay, run_drive), reverse=backward, a...]
    unnamed x130 -> x129, local copies, waits for them, and re-layouts: 77.5 us -> 56 us
    slice x2, local copies, waits for them, and re-layouts: 22.9 us -> 1.89 us  [chained(): incoming = jnp.concatenate([inclusive[:, 1:], edge], axis=1)]
  transfers between devices with their start and end apart: 3 -> 5, of which waited for: 3 -> 5; matrix products, arithmetic and copies ran while one was open for 5% -> 6% of each run, Pallas kernels for 0% -> 0%
where the time goes in v1:
time: 888 us; the launch traced here: 882 us
  waiting for transfers between devices  383 us (43%)
  other arithmetic  148 us (17%)
  local copies, waits for them, and re-layouts  146 us (16%)
  blocking collectives  124 us (14%)
  matrix products  61.8 us (7%)
  between operations  16.8 us (2%)
    psum x1, waiting for transfers between devices, shards(): lax.psum((weight_grad, jnp.sum(dnormed * unit_slice, axis=0), jnp.sum(dno...  229 us
    reduce_scatter x1, waiting for transfers between devices, shards(): lax.psum_scatter(partial_in, 'gate', scatter_dimension=1, tiled=True)  89.1 us
    all_to_all x1, blocking collectives, shards(): lax.all_to_all(dstreams, 'gate', split_axis=1, concat_axis=1, tiled=True)  74.2 us
    ppermute x3, waiting for transfers between devices, exchange_in_pairs(): part = lax.ppermute(part, axis, [(d, d ^ mask) for d in range(ways)])  64.2 us
    unnamed x129, local copies, waits for them, and re-layouts  56 us
    dot_general x2, matrix products, contract(): lax.dot_general(left, right, (((left_dim,), (right_dim,)), ((), ())), pre...  43.6 us
    psum x1, blocking collectives, shards(): lax.psum((weight_grad, jnp.sum(dnormed * unit_slice, axis=0), jnp.sum(dno...  39.2 us
    another operation x9, other arithmetic, chained(): jnp.stack([part_drive[step] + part_decay[step] * incoming for step in ran...  33.3 us
  transfers between devices with their start and end apart: 5, of which 5 were waited for; matrix products, arithmetic and copies ran while one was open for 6% of the time, Pallas kernels for 0%

profile of v1, /device:TPU:0, one launch (start us, length us, event | category | flops | bytes accessed | tf_op | source)
XLA Modules:
  0.0 881.9 jit_solution(8359658109291107222)
XLA Ops:
  8.1 4.7 convert_reduce_fusion
  12.8 1.1 copy-done
  13.8 2.3 fusion.3
  16.2 18.2 %fusion.18 = bf16[2048,1536]{1,0:T(8,128)(2,1)S(1)} fusion(bf16[2048,1536]{1,0:T(8,128)(2,1)} %param.12, f32[2048]{0:T(1024)S(1)} %copy-done.61, f32[2048]{0:T(1024)S(1)} %copy-done.59, bf16[1,2048,2048]{2,1,0:T(8,128)(2,1)} %param.11, f32[2048]{0:T(1024)S(1)} %add_rsqrt_fusion, f32[2048]{0:T(1024)S(1)} %broadcast_multiply_fusion.2), kind=kOutput, calls=%fused_computation.27 | convolution fusion | flops 12913213440 | bytes 21004288 | tf_op jit(solution)/shard_map/dot_general | solution.py:91
  34.5 3.0 broadcast_in_dim.6
  37.5 2.9 constant_dynamic-slice_fusion
  40.9 2.6 collective-permute-start.1
  43.6 0.6 collective-permute-done
  44.3 2.9 constant_dynamic-update-slice_fusion.2
  47.2 31.7 %collective-permute-done.1 = bf16[2048,384]{1,0:T(8,128)(2,1)S(1)} collective-permute-done((bf16[2048,384]{1,0:T(8,128)(2,1)}, bf16[2048,384]{1,0:T(8,128)(2,1)S(1)}, u32[]{:S(2)}, u32[]{:S(2)}) %collective-permute-start.1) | collective-permute-done | bytes 1572896 | tf_op jit(solution)/shard_map/ppermute | solution.py:21
  78.9 1.5 constant_dynamic-update-slice_fusion.1
  80.4 31.9 %collective-permute-done.2 = bf16[2048,384]{1,0:T(8,128)(2,1)S(1)} collective-permute-done((bf16[2048,384]{1,0:T(8,128)(2,1)}, bf16[2048,384]{1,0:T(8,128)(2,1)S(1)}, u32[]{:S(2)}, u32[]{:S(2)}) %collective-permute-start.2) | collective-permute-done | bytes 1572896 | tf_op jit(solution)/shard_map/ppermute | solution.py:21
  112.3 1.4 constant_dynamic-update-slice_fusion
  113.7 7.8 convert_multiply_fusion.5
  122.0 1.5 copy-done.1
  124.0 4.4 fusion.93
  128.4 7.3 fusion.46
  138.3 0.7 fusion.110
  139.1 0.7 slice.760
  139.8 0.7 slice.706
  141.0 16.8 %fusion.78 = (f32[1,128,512]{2,0,1:T(1,128)S(1)}, f32[1,128,512]{2,0,1:T(1,128)}, f32[1,128,512]{2,0,1:T(1,128)}, f32[1,128,512]{2,0,1:T(1,128)}, f32[1,128,512]...) fusion(f32[16,1,128,512]{3,0,2,1:T(8,128)} %bitcast.776), kind=kLoop, calls=%fused_computation.197 | loop fusion | flops 983040 | bytes 6029312 | tf_op jit(solution)/shard_map/mul | solution.py:46
  157.9 15.9 %fusion.62 = (f32[1,128,512]{2,0,1:T(1,128)S(1)}, f32[1,128,512]{2,0,1:T(1,128)}, f32[1,128,512]{2,0,1:T(1,128)}, f32[1,128,512]{2,0,1:T(1,128)}, f32[1,128,512]...) fusion(f32[16,1,128,512]{3,0,2,1:T(8,128)} %bitcast.787, ...), kind=kLoop, calls=%fused_computation.118 | loop fusion | flops 2097152 | bytes 10485760 | tf_op jit(solution)/shard_map/add | solution.py:47
  176.9 0.9 fusion.109
  177.8 0.9 pad_maximum_fusion.4
  179.7 19.6 %pad.211 = f32[1,128,512]{2,0,1:T(1,128)} pad(f32[1,64,512]{2,0,1:T(1,128)S(1)} %add.1800, f32[]{:T(128)} %constant.16.clone.1), padding=0_0_0x1_0_1x0_0_0 | pad | bytes 393220
  199.3 1.2 fusion.108
  200.5 0.8 pad_maximum_fusion.2
  201.3 0.9 pad.149
  202.2 1.9 slice_add_fusion.15
  204.1 1.0 slice.763
  205.1 19.6 %pad.210 = f32[1,128,512]{2,0,1:T(1,128)} pad(f32[1,64,512]{2,0,1:T(1,128)S(1)} %add.1747, f32[]{:T(128)} %constant.16.clone.1), padding=0_0_0x1_0_1x0_0_0 | pad | bytes 393220
  224.7 1.0 pad_maximum_fusion.1
  225.7 19.5 %pad.147 = f32[1,127,512]{2,0,1:T(1,128)} pad(f32[1,64,512]{2,0,1:T(1,128)S(1)} %pad_maximum_fusion.1, f32[]{:T(128)} %constant.16.clone.1), padding=0_0_0x0_0_1x0_0_0 | pad | bytes 391172 | tf_op jit(solution)/shard_map/slice | solution.py:55
  245.2 1.4 slice_add_fusion.16
  246.6 7.0 add_bitcast_fusion.17
  253.7 3.4 add_bitcast_fusion.16
  257.1 1.9 add_bitcast_fusion.18
  259.0 5.1 add_bitcast_fusion.19
  264.2 3.0 add_bitcast_fusion.4
  267.2 2.2 add_bitcast_fusion.3
  269.4 3.2 add_bitcast_fusion
  272.7 3.2 add_bitcast_fusion.10
  275.9 4.3 add_bitcast_fusion.21
  280.3 12.9 %stack.135 = f32[16,1,128,512]{3,0,2,1:T(8,128)} concatenate(f32[1,1,128,512]{3,0,2,1:T(1,128)} %get-tuple-element.135, f32[1,1,128,512]{3,0,2,1:T(1,128)} %get-tuple-element.69, f32[1,1,128,512]{3,0,2,1:T(1,128)} %get-tuple-element.84, f32[1,1,128,512]{3,0,2,1:T(1,128)S(1)} %copy-done.37, f32[1,1,128,512]{3,0,2,1:T(1,128)S(1)} %copy-done.40, ...), dimensions={0} | concatenate | bytes 8388608 | tf_op jit(solution)/shard_map/stack | solution.py:56
  293.4 13.0 %stack.118 = f32[16,1,128,512]{3,0,2,1:T(8,128)} concatenate(f32[1,1,128,512]{3,0,2,1:T(1,128)} %get-tuple-element.77, f32[1,1,128,512]{3,0,2,1:T(1,128)} %get-tuple-element.83, f32[1,1,128,512]{3,0,2,1:T(1,128)} %get-tuple-element.74, f32[1,1,128,512]{3,0,2,1:T(1,128)S(1)} %copy-done.35, f32[1,1,128,512]{3,0,2,1:T(1,128)S(1)} %copy-done.33, ...), dimensions={0} | concatenate | bytes 8388608 | tf_op jit(solution)/shard_map/stack | solution.py:56
  306.4 13.0 %fusion.41 = (f32[512]{0:T(512)S(1)}, f32[512]{0:T(512)S(1)}, f32[512]{0:T(512)S(1)}, f32[512]{0:T(512)S(1)}, f32[1,2048,512]{2,1,0:T(8,128)S(1)}, /*index=5*/f3...) fusion(bf16[1,2048,2048]{2,1,0:T(8,128)(2,1)} %param.11, s32[]{:T(128)S(6)} %select_n.25, ...), kind=kLoop, calls=%fused_computation.53 | loop fusion | flops 44038144 | bytes 35682308 | tf_op jit(solution)/shard_map/reduce_sum | solution.py:148
  320.0 1.4 copy-done.6
  321.4 1.4 copy-done.7
  322.8 2.9 pad_maximum_fusion
  325.8 11.4 %convert_element_type.48 = bf16[2048,4,384]{2,1,0:T(4,128)(2,1)} reshape(bf16[1,2048,1536]{2,1,0:T(8,128)(2,1)} %pad_maximum_fusion) | data formatting | bytes 12582912 | tf_op jit(solution)/shard_map/convert_element_type | solution.py:120
  337.2 3.6 copy.21
  340.8 74.2 %all_to_all.9 = bf16[2048,4,384]{2,0,1:T(8,128)(2,1)} all-to-all(bf16[2048,4,384]{2,0,1:T(8,128)(2,1)S(1)} %copy.21), channel_id=1, replica_groups=mesh['dp'=8,'gate'=4] {'gate'}, dimensions={1} | all-to-all | bytes 12582912 | tf_op jit(solution)/shard_map/all_to_all | solution.py:122
  415.0 8.7 copy.22
  423.7 20.6 %fusion.159 = f32[2048,2048]{1,0:T(8,128)} fusion(bf16[2048,1536]{0,1:T(8,128)(2,1)} %bitcast.795, bf16[2048,1536]{1,0:T(8,128)(2,1)} %param.12), kind=kOutput, calls=%fused_computation.317 | convolution fusion | flops 12884901888 | bytes 29360128 | tf_op jit(solution)/shard_map/dot_general | solution.py:63
  444.3 0.6 copy-done.45
  445.0 23.0 %fusion.10 = f32[2048,1536]{1,0:T(8,128)} fusion(bf16[2048,1536]{0,1:T(8,128)(2,1)} %bitcast.796, bf16[1,2048,2048]{2,1,0:T(8,128)(2,1)} %param.11, f32[2048]{0:T(1024)S(1)} %copy-done.62, f32[2048]{0:T(1024)S(1)} %copy-done.60, f32[2048]{0:T(1024)S(1)} %copy-done.45, f32[2048]{0:T(1024)S(1)} %copy-done.47), kind=kOutput, calls=%fused_computation.20 | convolution fusion | flops 12910067712 | bytes 27295744 | tf_op jit(solution)/shard_map/dot_general | solution.py:63
  468.1 12.3 %fusion.1 = f32[2048,2048]{1,0:T(8,128)} fusion(bf16[1,2048,2048]{2,1,0:T(8,128)(2,1)} %param.11, f32[2048]{0:T(1024)S(1)} %copy-done.45, f32[2048]{0:T(1024)S(1)} %copy-done.47), kind=kLoop, calls=%fused_computation.4 | loop fusion | flops 12582912 | bytes 25182208 | tf_op jit(solution)/shard_map/mul | solution.py:89
  480.4 89.1 %reduce-scatter.2.cloned.1.call-done = f32[2048,512]{1,0:T(8,128)} async-done(((f32[2048,2048]{1,0:T(8,128)}), f32[2048,512]{1,0:T(8,128)}) %reduce-scatter.2.cloned.1.call-update) | async-done | bytes 4194320 | tf_op jit(solution)/shard_map/reduce_scatter | solution.py:125
  569.5 5.1 multiply_reduce_fusion
  574.6 39.2 %all-reduce.32 = (f32[512]{0:T(512)}, f32[512]{0:T(512)}, f32[512]{0:T(512)}, f32[512]{0:T(512)}, f32[512]{0:T(512)}, /*index=5*/f32[512]{0:T(512)}) all-reduce(f32[512]{0:T(512)S(1)} %get-tuple-element.9, f32[512]{0:T(512)S(1)} %get-tuple-element.16, f32[512]{0:T(512)S(1)} %get-tuple-element.12, ...), channel_id=1, replica_groups=mesh['dp'=8,'gate'=4] {'dp'}, use_global_device_ids=true, to_apply=%region_9.0 | all-reduce | flops 3072 | bytes 24576 | tf_op jit(solution)/shard_map/psum | solution.py:142
  613.8 10.4 %all-reduce.33 = (f32[2048]{0:T(1024)S(1)}, f32[2048,1]{0,1:T(1,128)S(1)}) all-reduce(f32[2048]{0:T(1024)S(1)} %get-tuple-element.10, f32[2048,1]{0,1:T(1,128)S(1)} %bitcast.803), channel_id=1, replica_groups=mesh['dp'=8,'gate'=4] {'gate'}, use_global_device_ids=true, to_apply=%region_6.0 | all-reduce | flops 4096 | bytes 32768 | tf_op jit(solution)/shard_map/psum | solution.py:129
  624.2 10.1 %fusion.45 = bf16[1,2048,512]{2,1,0:T(8,128)(2,1)} fusion(f32[1,2048,512]{2,1,0:T(8,128)} %copy-done.7, f32[512]{0:T(512)S(1)} %copy-done.54, f32[1,2048,512]{2,1,0:T(8,128)} %copy-done.6, f32[512]{0:T(512)S(1)} %copy-done.50, f32[2048]{0:T(1024)S(1)} %bitcast.799, bf16[1,2048,512]{2,1,0:T(8,128)(2,1)S(1)} %copy-done.11, f32[2048]{0:T(1024)S(1)} %get-tuple-element.23, ...), kind=kLoop, calls=%fused_computation.67 | loop fusion | flops 25165824 | bytes 25206788 | tf_op jit(solution)/shard_map/reshape | solution.py:140
  634.3 229.3 %all-reduce.36.cloned.1.call-done = f32[2048,1536]{1,0:T(8,128)} async-done(((f32[2048,1536]{1,0:T(8,128)}), f32[2048,1536]{1,0:T(8,128)}) %all-reduce.36.cloned.1.call-update) | async-done | bytes 12582928 | tf_op jit(solution)/shard_map/psum | solution.py:142
  863.6 10.6 %copy.28 = f32[2048,1536]{1,0:T(8,128)} copy(f32[2048,1536]{1,0:T(8,128)} %all-reduce.36.cloned.1.call-done) | data formatting | bytes 25165824
  (213 shorter events, 9.7 us)
Async XLA Ops:
  8.0 561.5 %reduce-scatter.2.cloned.1.call-start = ((), (), s32[]{:S(2)}) async-start(), calls=%async_computation.2 | async-start | bytes 20971520 | tf_op jit(solution)/shard_map/reduce_scatter | solution.py:125
  8.1 5.8 copy-start
  13.8 2.4 copy-start.46
  13.8 2.4 copy-start.59
  13.8 2.4 copy-start.61
  16.2 18.3 %copy-start.44 = (f32[2048]{0:T(1024)}, f32[2048]{0:T(1024)S(1)}, u32[]{:S(2)}) copy-start(f32[2048]{0:T(1024)S(1)} %add_rsqrt_fusion) | copy-start | bytes 24580
  37.5 6.1 copy-start.55
  37.5 6.2 copy-start.56
  40.4 3.9 collective-permute-start
  40.9 38.0 %collective-permute-start.1 = (bf16[2048,384]{1,0:T(8,128)(2,1)}, bf16[2048,384]{1,0:T(8,128)(2,1)S(1)}, u32[]{:S(2)}, u32[]{:S(2)}) collective-permute-start(bf16[2048,384]{1,0:T(8,128)(2,1)} %get-tuple-element.79), channel_id=1, source_target_pairs={{0,2},{1,3},{2,0},{3,1},{4,6},{5,7},{6,4},{7,5},{8,10},{9,11},{10,... | collective-permute-start | bytes 4718600 | tf_op jit(solution)/shard_map/ppermute | solution.py:21
  43.5 68.8 %collective-permute-start.2 = (bf16[2048,384]{1,0:T(8,128)(2,1)}, bf16[2048,384]{1,0:T(8,128)(2,1)S(1)}, u32[]{:S(2)}, u32[]{:S(2)}) collective-permute-start(bf16[2048,384]{1,0:T(8,128)(2,1)} %get-tuple-element.78), channel_id=1, source_target_pairs={{0,3},{1,2},{2,1},{3,0},{4,7},{5,6},{6,5},{7,4},{8,11},{9,10},{10,... | collective-permute-start | bytes 4718600 | tf_op jit(solution)/shard_map/ppermute | solution.py:21
  43.6 70.0 %copy-start.42 = (f32[1,2048]{1,0:T(1,128)}, f32[1,2048]{1,0:T(1,128)S(1)}, u32[]{:S(2)}) copy-start(f32[1,2048]{1,0:T(1,128)S(1)} %convert_element_type.40) | copy-start | bytes 24580
  43.6 70.0 %copy-start.48 = (f32[1,2048]{1,0:T(1,128)}, f32[1,2048]{1,0:T(1,128)S(1)}, u32[]{:S(2)}) copy-start(f32[1,2048]{1,0:T(1,128)S(1)} %subtract_convert_fusion) | copy-start | bytes 24580
  44.3 69.4 %copy-start.10 = (bf16[1,2048,512]{2,1,0:T(8,128)(2,1)S(1)}, bf16[1,2048,512]{2,1,0:T(8,128)(2,1)}, u32[]{:S(2)}) copy-start(bf16[1,2048,512]{2,1,0:T(8,128)(2,1)} %param.21) | copy-start | bytes 6291460
  44.3 69.4 %copy-start.50 = (f32[512]{0:T(512)S(1)}, f32[512]{0:T(512)}, u32[]{:S(2)}) copy-start(f32[512]{0:T(512)} %param.15) | copy-start | bytes 6148
  44.3 69.4 %copy-start.51 = (f32[512]{0:T(512)S(1)}, f32[512]{0:T(512)}, u32[]{:S(2)}) copy-start(f32[512]{0:T(512)} %param.18) | copy-start | bytes 6148
  44.3 69.4 %copy-start.53 = (f32[512]{0:T(512)S(1)}, f32[512]{0:T(512)}, u32[]{:S(2)}) copy-start(f32[512]{0:T(512)} %param.16) | copy-start | bytes 6148
  44.3 69.4 %copy-start.57 = (f32[512]{0:T(512)S(1)}, f32[512]{0:T(512)}, u32[]{:S(2)}) copy-start(f32[512]{0:T(512)} %param.17) | copy-start | bytes 6148
  121.5 2.1 copy-start.1
  121.5 6.9 copy-start.8
  124.0 11.7 %copy-start.4 = (f32[1,2048,512]{2,1,0:T(8,128)}, f32[1,2048,512]{2,1,0:T(8,128)S(1)}, u32[]{:S(2)}) copy-start(f32[1,2048,512]{2,1,0:T(8,128)S(1)} %concatenate.59) | copy-start | bytes 12582916
  138.3 19.6 %copy-start.2 = (f32[1,2048,512]{2,1,0:T(8,128)S(1)}, f32[1,2048,512]{2,1,0:T(8,128)}, u32[]{:S(2)}) copy-start(f32[1,2048,512]{2,1,0:T(8,128)} %copy-done.1) | copy-start | bytes 12582916
  157.9 95.8 %copy-start.19 = (f32[1,128,512]{2,0,1:T(1,128)}, f32[1,128,512]{2,0,1:T(1,128)S(1)}, u32[]{:S(2)}) copy-start(f32[1,128,512]{2,0,1:T(1,128)S(1)} %get-tuple-element.47) | copy-start | bytes 786436
  173.7 79.9 %copy-start.20 = (f32[1,128,512]{2,0,1:T(1,128)}, f32[1,128,512]{2,0,1:T(1,128)S(1)}, u32[]{:S(2)}) copy-start(f32[1,128,512]{2,0,1:T(1,128)S(1)} %get-tuple-element.54) | copy-start | bytes 786436
  245.2 11.9 %copy-start.21 = (f32[1,128,512]{2,0,1:T(1,128)S(1)}, f32[1,128,512]{2,0,1:T(1,128)}, u32[]{:S(2)}) copy-start(f32[1,128,512]{2,0,1:T(1,128)} %get-tuple-element.44) | copy-start | bytes 786436
  245.2 11.9 %copy-start.22 = (f32[1,128,512]{2,0,1:T(1,128)S(1)}, f32[1,128,512]{2,0,1:T(1,128)}, u32[]{:S(2)}) copy-start(f32[1,128,512]{2,0,1:T(1,128)} %get-tuple-element.43) | copy-start | bytes 786436
  245.2 12.0 %copy-start.23 = (f32[1,128,512]{2,0,1:T(1,128)S(1)}, f32[1,128,512]{2,0,1:T(1,128)}, u32[]{:S(2)}) copy-start(f32[1,128,512]{2,0,1:T(1,128)} %get-tuple-element.51) | copy-start | bytes 786436
  245.2 12.0 %copy-start.24 = (f32[1,128,512]{2,0,1:T(1,128)S(1)}, f32[1,128,512]{2,0,1:T(1,128)}, u32[]{:S(2)}) copy-start(f32[1,128,512]{2,0,1:T(1,128)} %get-tuple-element.50) | copy-start | bytes 786436
  246.6 17.5 %copy-start.9 = (f32[1,2048,512]{2,1,0:T(8,128)S(1)}, f32[1,2048,512]{2,1,0:T(8,128)}, u32[]{:S(2)}) copy-start(f32[1,2048,512]{2,1,0:T(8,128)} %copy-done.8) | copy-start | bytes 12582916
  253.6 5.4 copy-start.3
  253.7 5.4 copy-start.18
  257.0 7.1 copy-start.5
  257.0 7.1 copy-start.12
  257.0 7.1 copy-start.13
  257.1 7.1 copy-start.14
  257.1 7.1 copy-start.15
  257.1 7.1 copy-start.16
  257.1 7.1 copy-start.17
  264.1 5.3 copy-start.27
  264.1 5.3 copy-start.28
  267.2 5.5 copy-start.25
  267.2 5.5 copy-start.26
  269.4 6.5 copy-start.29
  269.4 6.5 copy-start.30
  272.6 7.6 copy-start.36
  272.6 7.6 copy-start.37
  272.6 7.6 copy-start.38
  272.6 7.6 copy-start.39
  272.7 7.6 copy-start.40
  272.7 7.6 copy-start.41
  280.3 13.0 %copy-start.31 = (f32[1,1,128,512]{3,0,2,1:T(1,128)S(1)}, f32[1,1,128,512]{3,0,2,1:T(1,128)}, u32[]{:S(2)}) copy-start(f32[1,1,128,512]{3,0,2,1:T(1,128)} %get-tuple-element.70) | copy-start | bytes 786436
  280.3 13.0 %copy-start.32 = (f32[1,1,128,512]{3,0,2,1:T(1,128)S(1)}, f32[1,1,128,512]{3,0,2,1:T(1,128)}, u32[]{:S(2)}) copy-start(f32[1,1,128,512]{3,0,2,1:T(1,128)} %get-tuple-element.71) | copy-start | bytes 786436
  280.3 13.0 %copy-start.33 = (f32[1,1,128,512]{3,0,2,1:T(1,128)S(1)}, f32[1,1,128,512]{3,0,2,1:T(1,128)}, u32[]{:S(2)}) copy-start(f32[1,1,128,512]{3,0,2,1:T(1,128)} %get-tuple-element.72) | copy-start | bytes 786436
  280.3 13.0 %copy-start.34 = (f32[1,1,128,512]{3,0,2,1:T(1,128)S(1)}, f32[1,1,128,512]{3,0,2,1:T(1,128)}, u32[]{:S(2)}) copy-start(f32[1,1,128,512]{3,0,2,1:T(1,128)} %get-tuple-element.97) | copy-start | bytes 786436
  280.3 13.0 %copy-start.35 = (f32[1,1,128,512]{3,0,2,1:T(1,128)S(1)}, f32[1,1,128,512]{3,0,2,1:T(1,128)}, u32[]{:S(2)}) copy-start(f32[1,1,128,512]{3,0,2,1:T(1,128)} %get-tuple-element.98) | copy-start | bytes 786436
  293.3 13.0 %copy-start.11 = (bf16[1,2048,512]{2,1,0:T(8,128)(2,1)S(1)}, bf16[1,2048,512]{2,1,0:T(8,128)(2,1)}, u32[]{:S(2)}) copy-start(bf16[1,2048,512]{2,1,0:T(8,128)(2,1)} %param.21) | copy-start | bytes 6291460
  293.3 13.0 %copy-start.43 = (f32[1,2048]{1,0:T(1,128)S(1)}, f32[1,2048]{1,0:T(1,128)}, u32[]{:S(2)}) copy-start(f32[1,2048]{1,0:T(1,128)} %copy-done.42) | copy-start | bytes 24580
  293.3 13.0 %copy-start.49 = (f32[1,2048]{1,0:T(1,128)S(1)}, f32[1,2048]{1,0:T(1,128)}, u32[]{:S(2)}) copy-start(f32[1,2048]{1,0:T(1,128)} %copy-done.48) | copy-start | bytes 24580
  293.4 13.0 %copy-start.52 = (f32[512]{0:T(512)S(1)}, f32[512]{0:T(512)}, u32[]{:S(2)}) copy-start(f32[512]{0:T(512)} %param.18) | copy-start | bytes 6148
  293.4 13.0 %copy-start.54 = (f32[512]{0:T(512)S(1)}, f32[512]{0:T(512)}, u32[]{:S(2)}) copy-start(f32[512]{0:T(512)} %param.16) | copy-start | bytes 6148
  293.4 13.0 %copy-start.58 = (f32[512]{0:T(512)S(1)}, f32[512]{0:T(512)}, u32[]{:S(2)}) copy-start(f32[512]{0:T(512)} %param.17) | copy-start | bytes 6148
  319.4 2.0 copy-start.6
  319.4 3.4 copy-start.7
  444.3 419.3 %all-reduce.36.cloned.1.call-start = ((), (), s32[]{:S(2)}) async-start(), calls=%async_computation.3 | async-start | bytes 25165824 | tf_op jit(solution)/shard_map/psum | solution.py:142
  (4 other events, 2.9 us)
Sparse Core Ops, SparseCore 0:
  444.4 125.0 reduce-scatter.1
Sparse Core Ops, SparseCore 1:
  468.1 395.4 all-reduce.35
